TPU v7x, 128 devices: a whole 4x4x4 slice. The times are simulated.
128 devices in a mesh: tok: 8 (over x, core), voc: 16 (over z, y).
Axes of the slice: x: 4, y: 4, z: 4, core: 2. Of those that a mesh axis runs over, the one named last changes fastest.
Arguments:
- hidden: bfloat16 [256, 32, 2048], P(('tok', 'voc')), may hold values from -40 to 40
- norm_gain: float32 [2048], replicated, may hold values from 0.5 to 1.5
- head_weight: bfloat16 [2048, 102400], P(None, 'voc'), may hold values from -2 to 2
- lengths: int32 [256], P(('tok', 'voc')), may hold values from 12 to 24, as said below
- offsets: int32 [256], P(('tok', 'voc')), may hold values from 0 to 8
- slot_request: int32 [256], replicated, may hold values from 0 to 255, each once
- targets: int32 [256, 32], P(('tok', 'voc')), may hold values from 0 to 102399
Outputs:
- token_logprob: float32 [256, 32], P(('tok', 'voc'))
- token_entropy: float32 [256, 32], P(('tok', 'voc'))
Inputs may be any that keep to these rules, and one draw needn't show every extreme that they name: `lengths`: each request has 12 to 24 response rows; all 2 requests of some one scoring device have exactly 24. Response rows end within the window: offsets + lengths <= 32. `slot_request`: every request appears in exactly one slot.
All inputs are finite; a program needn't handle non-finite values.
Results may differ from a plain program's by a relative error of at most 0.00145.
Values may be sent and summed in bfloat16 or wider, within the bound.
A program may use at most 128 MiB of HBM per device.

v0:
```python
import jax
import jax.numpy as jnp
from jax import lax
from jax.sharding import PartitionSpec as P

EPS = 1e-06


def normalize(hidden, norm_gain):
    values = hidden.astype(jnp.float32)
    square = jnp.mean(values * values, axis=-1, keepdims=True)
    return (values * lax.rsqrt(square + EPS) * norm_gain).astype(jnp.bfloat16)


def shards(hidden, norm_gain, head_weight, lengths, offsets, slot_request, targets):
    req_dev, span, width = hidden.shape
    vocab_dev = head_weight.shape[1]
    normed = normalize(hidden, norm_gain).reshape(req_dev * span, width)
    position = jnp.arange(span, dtype=jnp.int32)[None, :]
    in_span = (
        (position >= offsets[:, None]) & (position < offsets[:, None] + lengths[:, None])
    ).reshape(-1)
    flat_targets = targets.reshape(-1)
    own_count = normed.shape[0]
    group_matrix, group_targets = (
        lax.all_gather(normed, "voc", axis=0, tiled=True),
        lax.all_gather(flat_targets, "voc", axis=0, tiled=True),
    )
    logits = jnp.dot(group_matrix, head_weight, preferred_element_type=jnp.float32)
    shard_index = lax.axis_index("voc")
    local_column = group_targets - shard_index * vocab_dev
    target_hit = jnp.arange(vocab_dev, dtype=jnp.int32)[None, :] == local_column[:, None]
    picked = jnp.sum(jnp.where(target_hit, logits, 0.0), axis=1)
    row_peak = jnp.max(logits, axis=1)
    scaled = jnp.exp(logits - row_peak[:, None])
    exp_sum = jnp.sum(scaled, axis=1)
    exp_dot = jnp.sum(scaled * logits, axis=1)
    first_row = shard_index * own_count
    peak_all = lax.pmax(row_peak, "voc")
    rescale = jnp.exp(row_peak - peak_all)
    sum_all, dot_all, pick_all = lax.psum((exp_sum * rescale, exp_dot * rescale, picked), "voc")
    peak_own = lax.dynamic_slice_in_dim(peak_all, first_row, own_count)
    sum_own = lax.dynamic_slice_in_dim(sum_all, first_row, own_count)
    dot_own = lax.dynamic_slice_in_dim(dot_all, first_row, own_count)
    pick_own = lax.dynamic_slice_in_dim(pick_all, first_row, own_count)
    log_total = jnp.log(sum_own)
    logprob = pick_own - peak_own - log_total
    entropy = peak_own + log_total - dot_own / sum_own
    logprob_rows = jnp.where(in_span, logprob, 0.0).reshape(req_dev, span)
    entropy_rows = jnp.where(in_span, entropy, 0.0).reshape(req_dev, span)
    device = lax.axis_index(("tok", "voc"))
    every_logprob, every_entropy = (
        lax.all_gather(logprob_rows, ("tok", "voc"), axis=0, tiled=True),
        lax.all_gather(entropy_rows, ("tok", "voc"), axis=0, tiled=True),
    )
    wanted = device * req_dev + jnp.arange(req_dev, dtype=jnp.int32)
    picking = slot_request[None, :] == wanted[:, None]
    token_logprob = jnp.sum(jnp.where(picking[:, :, None], every_logprob[None, :, :], 0.0), axis=1)
    token_entropy = jnp.sum(jnp.where(picking[:, :, None], every_entropy[None, :, :], 0.0), axis=1)
    return (token_logprob, token_entropy)


def solution(mesh):
    placed = (
        P(("tok", "voc"), None, None),
        P(),
        P(None, "voc"),
        P(("tok", "voc")),
        P(("tok", "voc")),
        P(),
        P(("tok", "voc"), None),
    )
    return jax.shard_map(
        shards,
        mesh=mesh,
        in_specs=placed,
        out_specs=(P(("tok", "voc"), None), P(("tok", "voc"), None)),
        check_vma=False,
    )
```

profile of v0, /device:TPU:0, one launch (start us, length us, event | category | flops | bytes accessed | tf_op | source)
XLA Modules:
  0.0 326.7 jit_solution(2216714420504681096)
XLA Ops:
  7.2 0.0 all-gather.4.cloned.1.call-start
  7.2 1.1 fusion.1
  8.3 1.8 fusion.3
  10.1 0.0 all-gather.4.cloned.1.call-update
  10.1 0.7 add.46
  10.8 0.7 compare_and_fusion
  11.5 0.1 and.10
  11.6 0.8 reshape.74
  12.4 1.2 dynamic-slice
  14.3 0.2 dynamic-update-slice
  14.5 17.9 %all-reduce = s32[1024]{0:T(1024)S(1)} all-reduce(s32[1024]{0:T(1024)S(1)} %dynamic-update-slice), channel_id=1, replica_groups=mesh['tok'=8,'voc'=16] {'voc'}, use_global_device_ids=true, to_apply=%add | all-reduce | flops 1024 | bytes 8192
  32.4 0.8 broadcast_compare_fusion
  33.2 31.1 %all-gather.4.cloned.1.call-done = bf16[1024,2048]{1,0:T(8,128)(2,1)} async-done(((bf16[64,2048]{1,0:T(8,128)(2,1)}), bf16[1024,2048]{1,0:T(8,128)(2,1)}) %all-gather.4.cloned.1.call-update) | async-done | bytes 4194320 | tf_op jit(solution)/shard_map/all_gather | solution.py:26
  64.3 34.9 %fusion.6 = (f32[1024]{0:T(1024)S(1)}, f32[1024,6400]{1,0:T(8,128)}) fusion(bf16[1024,2048]{1,0:T(8,128)(2,1)} %all-gather.4.cloned.1.call-done, bf16[2048,6400]{1,0:T(8,128)(2,1)} %param.9), kind=kOutput, calls=%fused_computation.22 | convolution fusion | flops 26850099200 | bytes 56627200 | tf_op jit(solution)/shard_map/dot_general | solution.py:29
  99.2 38.5 %pmax.7 = f32[1024]{0:T(1024)S(1)} all-reduce(f32[1024]{0:T(1024)S(1)} %get-tuple-element.14), channel_id=1, replica_groups=mesh['tok'=8,'voc'=16] {'voc'}, use_global_device_ids=true, to_apply=%region_4.5 | all-reduce | flops 1024 | bytes 8192 | tf_op jit(solution)/shard_map/pmax | solution.py:39
  137.7 11.4 %multiply_reduce_fusion = (f32[1024]{0:T(1024)S(1)}, f32[1024]{0:T(1024)S(1)}, f32[1024]{0:T(1024)S(1)}) fusion(f32[1024,6400]{1,0:T(8,128)} %get-tuple-element.15, f32[1024]{0:T(1024)S(1)} %get-tuple-element.14, s32[1024]{0:T(1024)S(1)} %broadcast_subtract_fusion), kind=kLoop, calls=%fused_computation | loop fusion | flops 45872128 | bytes 26234880 | tf_op jit(solution)/shard_map/reduce_sum | solution.py:37
  149.1 69.6 %all-reduce.1 = (f32[1024]{0:T(1024)S(1)}, f32[1024]{0:T(1024)S(1)}, f32[1024]{0:T(1024)S(1)}) all-reduce(f32[1024]{0:T(1024)S(1)} %get-tuple-element.13, f32[1024]{0:T(1024)S(1)} %get-tuple-element.12, f32[1024]{0:T(1024)S(1)} %get-tuple-element.4), channel_id=1, replica_groups=mesh['tok'=8,'voc'=16] {'voc'}, use_global_device_ids=true, to_apply=%region_9.10 | all-reduce | flops 3072 | bytes 24576 | tf_op jit(solution)/shard_map/psum | solution.py:41
  218.7 0.1 subtract_select_fusion.1
  218.8 0.1 reshape.79
  218.9 49.9 %all-gather.1 = f32[128,2,32]{2,1,0:T(2,128)S(1)} all-gather(f32[1,2,32]{2,1,0:T(2,128)S(1)} %reshape.79), channel_id=1, replica_groups=mesh['tok'=8,'voc'=16] {'tok','voc'}, dimensions={0}, use_global_device_ids=true | all-gather | bytes 33024 | tf_op jit(solution)/shard_map/all_gather | solution.py:54
  268.8 0.1 copy.10
  268.8 0.1 reshape.77
  268.9 50.2 %all-gather = f32[128,2,32]{2,1,0:T(2,128)S(1)} all-gather(f32[1,2,32]{2,1,0:T(2,128)S(1)} %reshape.77), channel_id=1, replica_groups=mesh['tok'=8,'voc'=16] {'tok','voc'}, dimensions={0}, use_global_device_ids=true | all-gather | bytes 33024 | tf_op jit(solution)/shard_map/all_gather | solution.py:53
  319.1 0.1 copy.9
  319.2 0.7 select_reduce_fusion.1
  (5 shorter events, 0.0 us)
Async XLA Ops:
  7.2 57.1 %all-gather.4.cloned.1.call-start = ((), (), s32[]{:S(2)}) async-start(), calls=%async_computation | async-start | bytes 4456448 | tf_op jit(solution)/shard_map/all_gather | solution.py:26
Sparse Core Ops, SparseCore 0:
  10.2 53.9 all-gather.3
where the time goes:
time: 327 us
  blocking collectives  226 us (69%)
  matrix products  34.9 us (11%)
  waiting for transfers between devices  31.1 us (10%)
  other arithmetic  17.2 us (5%)
  between operations  14.7 us (4%)
    psum x1, blocking collectives, shards(): lax.psum((exp_sum * rescale, exp_dot * rescale, picked), 'voc')  69.6 us
    all_gather x1, blocking collectives, shards(): lax.all_gather(logprob_rows, ('tok', 'voc'), axis=0, tiled=True)  50.2 us
    all_gather x1, blocking collectives, shards(): lax.all_gather(entropy_rows, ('tok', 'voc'), axis=0, tiled=True)  49.9 us
    pmax x1, blocking collectives, shards(): peak_all = lax.pmax(row_peak, 'voc')  38.5 us
    dot_general x1, matrix products, shards(): jnp.dot(group_matrix, head_weight, preferred_element_type=jnp.float32)  34.9 us
    all_gather x1, waiting for transfers between devices, shards(): lax.all_gather(normed, 'voc', axis=0, tiled=True)  31.1 us
    unnamed x1, blocking collectives  17.9 us
    reduce_sum x1, other arithmetic, shards(): exp_dot = jnp.sum(scaled * logits, axis=1)  11.4 us
  transfers between devices with their start and end apart: 1, of which 1 were waited for; matrix products, arithmetic and copies ran while one was open for 1% of the time, Pallas kernels for 0%

commit v1 on v0

--- a/solution.py
+++ b/solution.py
@@ -4,6 +4,27 @@
 from jax.sharding import PartitionSpec as P
 
 EPS = 1e-06
+
+
+def gather_around(x, axis, dim):
+    size, place, rows = (lax.axis_size(axis), lax.axis_index(axis), x.shape[dim])
+    right = [(i, (i + 1) % size) for i in range(size)]
+    downward = [(i, (i - 1) % size) for i in range(size)]
+    result = jnp.zeros((*x.shape[:dim], size * rows, *x.shape[dim + 1 :]), x.dtype)
+    result = lax.dynamic_update_slice_in_dim(result, x, place * rows, axis=dim)
+    from_left = from_right = x
+    middle = size // 2
+    for turn in range(1, middle + 1):
+        from_left = lax.ppermute(from_left, axis, right)
+        result = lax.dynamic_update_slice_in_dim(
+            result, from_left, (place - turn) % size * rows, axis=dim
+        )
+        if turn < size - middle:
+            from_right = lax.ppermute(from_right, axis, downward)
+            result = lax.dynamic_update_slice_in_dim(
+                result, from_right, (place + turn) % size * rows, axis=dim
+            )
+    return result
 
 
 def normalize(hidden, norm_gain):
@@ -23,7 +44,7 @@
     flat_targets = targets.reshape(-1)
     own_count = normed.shape[0]
     group_matrix, group_targets = (
-        lax.all_gather(normed, "voc", axis=0, tiled=True),
+        gather_around(normed, "voc", 0),
         lax.all_gather(flat_targets, "voc", axis=0, tiled=True),
     )
     logits = jnp.dot(group_matrix, head_weight, preferred_element_type=jnp.float32)

time: 327 us -> 358 us (1.095)
  starting transfers between devices: 0.04 us -> 40.6 us
  between operations: 14.7 us -> 1.45 us
  waiting for transfers between devices: 31.1 us -> 41.2 us
  blocking collectives: 226 us -> 220 us
    ppermute x0 -> x15, waiting for transfers between devices: none -> 41.2 us  [the longest x8 40.9 us: gather_around(): from_left = lax.ppermute(from_left, axis, right)]
    ppermute x0 -> x15, starting transfers between devices: none -> 40.6 us  [the longest x7 38 us: gather_around(): from_right = lax.ppermute(from_right, axis, downward)]
    all_gather x1 -> x0, waiting for transfers between devices: 31.1 us -> none  [shards(): lax.all_gather(normed, 'voc', axis=0, tiled=True)]
    unnamed x1, blocking collectives: 17.9 us -> 13.2 us
  transfers between devices with their start and end apart: 1 -> 15, of which waited for: 1 -> 9; matrix products, arithmetic and copies ran while one was open for 1% -> 1% of each run, Pallas kernels for 0% -> 0%
where the time goes in v1:
time: 358 us; the launch traced here: 357 us
  blocking collectives  220 us (61%)
  waiting for transfers between devices  41.2 us (12%)
  starting transfers between devices  40.6 us (11%)
  matrix products  33.7 us (9%)
  other arithmetic  16.8 us (5%)
    psum x1, blocking collectives, shards(): lax.psum((exp_sum * rescale, exp_dot * rescale, picked), 'voc')  71.4 us
    all_gather x1, blocking collectives, shards(): lax.all_gather(logprob_rows, ('tok', 'voc'), axis=0, tiled=True)  50.2 us
    all_gather x1, blocking collectives, shards(): lax.all_gather(entropy_rows, ('tok', 'voc'), axis=0, tiled=True)  49.9 us
    ppermute x8, waiting for transfers between devices, gather_around(): from_left = lax.ppermute(from_left, axis, right)  40.9 us
    ppermute x7, starting transfers between devices, gather_around(): from_right = lax.ppermute(from_right, axis, downward)  38 us
    pmax x1, blocking collectives, shards(): peak_all = lax.pmax(row_peak, 'voc')  35.4 us
    dot_general x1, matrix products, shards(): jnp.dot(group_matrix, head_weight, preferred_element_type=jnp.float32)  33.7 us
    unnamed x1, blocking collectives  13.2 us
  transfers between devices with their start and end apart: 15, of which 9 were waited for; matrix products, arithmetic and copies ran while one was open for 1% of the time, Pallas kernels for 0%

profile of v1, /device:TPU:0, one launch (start us, length us, event | category | flops | bytes accessed | tf_op | source)
XLA Modules:
  0.0 357.3 jit_solution(1329275289332109252)
XLA Ops:
  0.6 1.1 fusion.1
  1.7 1.1 fusion.3
  2.8 1.8 collective-permute-start
  4.6 5.0 %collective-permute-start.1 = (bf16[64,2048]{1,0:T(8,128)(2,1)S(1)}, bf16[64,2048]{1,0:T(8,128)(2,1)S(1)}, u32[]{:S(2)}, u32[]{:S(2)}) collective-permute-start(bf16[64,2048]{1,0:T(8,128)(2,1)S(1)} %bitcast.7), channel_id=1, source_target_pairs={{0,15},{1,0},{2,1},{3,2},{4,3},{5,4},{6,5},{7,6},{8,7},{9,8},{10,9... | collective-permute-start | bytes 786440 | tf_op jit(solution)/shard_map/ppermute | solution.py:23
  9.6 0.8 reshape.74
  10.3 1.2 dynamic-slice
  12.2 0.2 dynamic-update-slice
  12.5 13.2 %all-reduce = s32[1024]{0:T(1024)S(1)} all-reduce(s32[1024]{0:T(1024)S(1)} %dynamic-update-slice), channel_id=1, replica_groups=mesh['tok'=8,'voc'=16] {'voc'}, use_global_device_ids=true, to_apply=%add | all-reduce | flops 1024 | bytes 8192
  25.7 0.7 add.167
  26.3 0.8 broadcast_compare_fusion
  27.1 0.7 compare_and_fusion
  27.8 0.1 and.71
  27.9 0.5 broadcast_in_dim.57
  28.5 0.0 collective-permute-done
  28.5 0.8 collective-permute-start.2
  29.2 0.0 collective-permute-done.1
  29.3 4.7 %collective-permute-start.3 = (bf16[64,2048]{1,0:T(8,128)(2,1)S(1)}, bf16[64,2048]{1,0:T(8,128)(2,1)S(1)}, u32[]{:S(2)}, u32[]{:S(2)}) collective-permute-start(bf16[64,2048]{1,0:T(8,128)(2,1)S(1)} %collective-permute-done.1), channel_id=1, source_target_pairs={{0,15},{1,0},{2,1},{3,2},{4,3},{5,4},{6,5},{7,6},{8,7},{9,8},{10,9... | collective-permute-start | bytes 786440 | tf_op jit(solution)/shard_map/ppermute | solution.py:23
  34.0 4.3 %collective-permute-done.2 = bf16[64,2048]{1,0:T(8,128)(2,1)S(1)} collective-permute-done((bf16[64,2048]{1,0:T(8,128)(2,1)S(1)}, bf16[64,2048]{1,0:T(8,128)(2,1)S(1)}, u32[]{:S(2)}, u32[]{:S(2)}) %collective-permute-start.2) | collective-permute-done | bytes 262176 | tf_op jit(solution)/shard_map/ppermute | solution.py:18
  38.2 0.0 collective-permute-start.4
  38.3 0.0 collective-permute-done.3
  38.3 5.3 %collective-permute-start.5 = (bf16[64,2048]{1,0:T(8,128)(2,1)S(1)}, bf16[64,2048]{1,0:T(8,128)(2,1)S(1)}, u32[]{:S(2)}, u32[]{:S(2)}) collective-permute-start(bf16[64,2048]{1,0:T(8,128)(2,1)S(1)} %collective-permute-done.3), channel_id=1, source_target_pairs={{0,15},{1,0},{2,1},{3,2},{4,3},{5,4},{6,5},{7,6},{8,7},{9,8},{10,9... | collective-permute-start | bytes 786440 | tf_op jit(solution)/shard_map/ppermute | solution.py:23
  43.7 4.6 %collective-permute-done.4 = bf16[64,2048]{1,0:T(8,128)(2,1)S(1)} collective-permute-done((bf16[64,2048]{1,0:T(8,128)(2,1)S(1)}, bf16[64,2048]{1,0:T(8,128)(2,1)S(1)}, u32[]{:S(2)}, u32[]{:S(2)}) %collective-permute-start.4) | collective-permute-done | bytes 262176 | tf_op jit(solution)/shard_map/ppermute | solution.py:18
  48.3 0.0 collective-permute-start.6
  48.3 0.0 collective-permute-done.5
  48.3 5.6 %collective-permute-start.7 = (bf16[64,2048]{1,0:T(8,128)(2,1)S(1)}, bf16[64,2048]{1,0:T(8,128)(2,1)S(1)}, u32[]{:S(2)}, u32[]{:S(2)}) collective-permute-start(bf16[64,2048]{1,0:T(8,128)(2,1)S(1)} %collective-permute-done.5), channel_id=1, source_target_pairs={{0,15},{1,0},{2,1},{3,2},{4,3},{5,4},{6,5},{7,6},{8,7},{9,8},{10,9... | collective-permute-start | bytes 786440 | tf_op jit(solution)/shard_map/ppermute | solution.py:23
  54.0 5.5 %collective-permute-done.6 = bf16[64,2048]{1,0:T(8,128)(2,1)S(1)} collective-permute-done((bf16[64,2048]{1,0:T(8,128)(2,1)S(1)}, bf16[64,2048]{1,0:T(8,128)(2,1)S(1)}, u32[]{:S(2)}, u32[]{:S(2)}) %collective-permute-start.6) | collective-permute-done | bytes 262176 | tf_op jit(solution)/shard_map/ppermute | solution.py:18
  59.5 0.0 collective-permute-start.8
  59.5 0.1 collective-permute-done.7
  59.6 5.8 %collective-permute-start.9 = (bf16[64,2048]{1,0:T(8,128)(2,1)S(1)}, bf16[64,2048]{1,0:T(8,128)(2,1)S(1)}, u32[]{:S(2)}, u32[]{:S(2)}) collective-permute-start(bf16[64,2048]{1,0:T(8,128)(2,1)S(1)} %collective-permute-done.7), channel_id=1, source_target_pairs={{0,15},{1,0},{2,1},{3,2},{4,3},{5,4},{6,5},{7,6},{8,7},{9,8},{10,9... | collective-permute-start | bytes 786440 | tf_op jit(solution)/shard_map/ppermute | solution.py:23
  65.5 6.4 %collective-permute-done.8 = bf16[64,2048]{1,0:T(8,128)(2,1)S(1)} collective-permute-done((bf16[64,2048]{1,0:T(8,128)(2,1)S(1)}, bf16[64,2048]{1,0:T(8,128)(2,1)S(1)}, u32[]{:S(2)}, u32[]{:S(2)}) %collective-permute-start.8) | collective-permute-done | bytes 262176 | tf_op jit(solution)/shard_map/ppermute | solution.py:18
  71.8 0.0 collective-permute-start.10
  71.8 0.2 collective-permute-done.9
  72.0 5.8 %collective-permute-start.11 = (bf16[64,2048]{1,0:T(8,128)(2,1)S(1)}, bf16[64,2048]{1,0:T(8,128)(2,1)S(1)}, u32[]{:S(2)}, u32[]{:S(2)}) collective-permute-start(bf16[64,2048]{1,0:T(8,128)(2,1)S(1)} %collective-permute-done.9), channel_id=1, source_target_pairs={{0,15},{1,0},{2,1},{3,2},{4,3},{5,4},{6,5},{7,6},{8,7},{9,8},{10,9... | collective-permute-start | bytes 786440 | tf_op jit(solution)/shard_map/ppermute | solution.py:23
  77.8 5.6 %collective-permute-done.10 = bf16[64,2048]{1,0:T(8,128)(2,1)S(1)} collective-permute-done((bf16[64,2048]{1,0:T(8,128)(2,1)S(1)}, bf16[64,2048]{1,0:T(8,128)(2,1)S(1)}, u32[]{:S(2)}, u32[]{:S(2)}) %collective-permute-start.10) | collective-permute-done | bytes 262176 | tf_op jit(solution)/shard_map/ppermute | solution.py:18
  83.5 0.0 collective-permute-start.12
  83.5 0.0 collective-permute-done.11
  83.5 5.8 %collective-permute-start.13 = (bf16[64,2048]{1,0:T(8,128)(2,1)S(1)}, bf16[64,2048]{1,0:T(8,128)(2,1)S(1)}, u32[]{:S(2)}, u32[]{:S(2)}) collective-permute-start(bf16[64,2048]{1,0:T(8,128)(2,1)S(1)} %collective-permute-done.11), channel_id=1, source_target_pairs={{0,15},{1,0},{2,1},{3,2},{4,3},{5,4},{6,5},{7,6},{8,7},{9,8},{10,9... | collective-permute-start | bytes 786440 | tf_op jit(solution)/shard_map/ppermute | solution.py:23
  89.4 4.9 %collective-permute-done.12 = bf16[64,2048]{1,0:T(8,128)(2,1)S(1)} collective-permute-done((bf16[64,2048]{1,0:T(8,128)(2,1)S(1)}, bf16[64,2048]{1,0:T(8,128)(2,1)S(1)}, u32[]{:S(2)}, u32[]{:S(2)}) %collective-permute-start.12) | collective-permute-done | bytes 262176 | tf_op jit(solution)/shard_map/ppermute | solution.py:18
  94.2 0.0 collective-permute-start.14
  94.3 0.0 collective-permute-done.13
  94.3 9.6 %collective-permute-done.14 = bf16[64,2048]{1,0:T(8,128)(2,1)S(1)} collective-permute-done((bf16[64,2048]{1,0:T(8,128)(2,1)S(1)}, bf16[64,2048]{1,0:T(8,128)(2,1)S(1)}, u32[]{:S(2)}, u32[]{:S(2)}) %collective-permute-start.14) | collective-permute-done | bytes 262176 | tf_op jit(solution)/shard_map/ppermute | solution.py:18
  104.0 33.7 %fusion.6 = (f32[1024]{0:T(1024)S(1)}, f32[1024,6400]{1,0:T(8,128)}) fusion(bf16[1024,2048]{1,0:T(8,128)(2,1)S(1)} %constant_dynamic-update-slice_fusion, bf16[2048,6400]{1,0:T(8,128)(2,1)} %param.9), kind=kOutput, calls=%fused_computation.38 | convolution fusion | flops 26850099200 | bytes 56627200 | tf_op jit(solution)/shard_map/dot_general | solution.py:50
  137.7 35.4 %pmax.7 = f32[1024]{0:T(1024)S(1)} all-reduce(f32[1024]{0:T(1024)S(1)} %get-tuple-element.14), channel_id=1, replica_groups=mesh['tok'=8,'voc'=16] {'voc'}, use_global_device_ids=true, to_apply=%region_4.5 | all-reduce | flops 1024 | bytes 8192 | tf_op jit(solution)/shard_map/pmax | solution.py:60
  173.1 11.7 %multiply_reduce_fusion = (f32[1024]{0:T(1024)S(1)}, f32[1024]{0:T(1024)S(1)}, f32[1024]{0:T(1024)S(1)}) fusion(f32[1024,6400]{1,0:T(8,128)} %get-tuple-element.15, f32[1024]{0:T(1024)S(1)} %get-tuple-element.14, s32[1024]{0:T(1024)S(1)} %broadcast_subtract_fusion), kind=kLoop, calls=%fused_computation | loop fusion | flops 45872128 | bytes 26234880 | tf_op jit(solution)/shard_map/reduce_sum | solution.py:58
  184.8 71.4 %all-reduce.1 = (f32[1024]{0:T(1024)S(1)}, f32[1024]{0:T(1024)S(1)}, f32[1024]{0:T(1024)S(1)}) all-reduce(f32[1024]{0:T(1024)S(1)} %get-tuple-element.13, f32[1024]{0:T(1024)S(1)} %get-tuple-element.12, f32[1024]{0:T(1024)S(1)} %get-tuple-element.4), channel_id=1, replica_groups=mesh['tok'=8,'voc'=16] {'voc'}, use_global_device_ids=true, to_apply=%region_9.10 | all-reduce | flops 3072 | bytes 24576 | tf_op jit(solution)/shard_map/psum | solution.py:62
  256.2 0.1 subtract_select_fusion.1
  256.3 0.1 reshape.79
  256.4 49.9 %all-gather.1 = f32[128,2,32]{2,1,0:T(2,128)S(1)} all-gather(f32[1,2,32]{2,1,0:T(2,128)S(1)} %reshape.79), channel_id=1, replica_groups=mesh['tok'=8,'voc'=16] {'tok','voc'}, dimensions={0}, use_global_device_ids=true | all-gather | bytes 33024 | tf_op jit(solution)/shard_map/all_gather | solution.py:75
  306.3 0.1 copy.10
  306.3 0.1 reshape.77
  306.4 50.2 %all-gather = f32[128,2,32]{2,1,0:T(2,128)S(1)} all-gather(f32[1,2,32]{2,1,0:T(2,128)S(1)} %reshape.77), channel_id=1, replica_groups=mesh['tok'=8,'voc'=16] {'tok','voc'}, dimensions={0}, use_global_device_ids=true | all-gather | bytes 33024 | tf_op jit(solution)/shard_map/all_gather | solution.py:74
  356.6 0.1 copy.9
  356.7 0.7 select_reduce_fusion.1
  (21 shorter events, 0.4 us)
Async XLA Ops:
  2.8 25.7 %collective-permute-start = (bf16[64,2048]{1,0:T(8,128)(2,1)S(1)}, bf16[64,2048]{1,0:T(8,128)(2,1)S(1)}, u32[]{:S(2)}, u32[]{:S(2)}) collective-permute-start(bf16[64,2048]{1,0:T(8,128)(2,1)S(1)} %bitcast.6), channel_id=1, source_target_pairs={{0,1},{1,2},{2,3},{3,4},{4,5},{5,6},{6,7},{7,8},{8,9},{9,10},{10,1... | collective-permute-start | bytes 786440 | tf_op jit(solution)/shard_map/ppermute | solution.py:18
  4.6 24.7 %collective-permute-start.1 = (bf16[64,2048]{1,0:T(8,128)(2,1)S(1)}, bf16[64,2048]{1,0:T(8,128)(2,1)S(1)}, u32[]{:S(2)}, u32[]{:S(2)}) collective-permute-start(bf16[64,2048]{1,0:T(8,128)(2,1)S(1)} %bitcast.7), channel_id=1, source_target_pairs={{0,15},{1,0},{2,1},{3,2},{4,3},{5,4},{6,5},{7,6},{8,7},{9,8},{10,9... | collective-permute-start | bytes 786440 | tf_op jit(solution)/shard_map/ppermute | solution.py:23
  28.5 9.8 %collective-permute-start.2 = (bf16[64,2048]{1,0:T(8,128)(2,1)S(1)}, bf16[64,2048]{1,0:T(8,128)(2,1)S(1)}, u32[]{:S(2)}, u32[]{:S(2)}) collective-permute-start(bf16[64,2048]{1,0:T(8,128)(2,1)S(1)} %collective-permute-done), channel_id=1, source_target_pairs={{0,1},{1,2},{2,3},{3,4},{4,5},{5,6},{6,7},{7,8},{8,9},{9,10},{10,1... | collective-permute-start | bytes 786440 | tf_op jit(solution)/shard_map/ppermute | solution.py:18
  29.3 9.0 %collective-permute-start.3 = (bf16[64,2048]{1,0:T(8,128)(2,1)S(1)}, bf16[64,2048]{1,0:T(8,128)(2,1)S(1)}, u32[]{:S(2)}, u32[]{:S(2)}) collective-permute-start(bf16[64,2048]{1,0:T(8,128)(2,1)S(1)} %collective-permute-done.1), channel_id=1, source_target_pairs={{0,15},{1,0},{2,1},{3,2},{4,3},{5,4},{6,5},{7,6},{8,7},{9,8},{10,9... | collective-permute-start | bytes 786440 | tf_op jit(solution)/shard_map/ppermute | solution.py:23
  38.2 10.0 %collective-permute-start.4 = (bf16[64,2048]{1,0:T(8,128)(2,1)S(1)}, bf16[64,2048]{1,0:T(8,128)(2,1)S(1)}, u32[]{:S(2)}, u32[]{:S(2)}) collective-permute-start(bf16[64,2048]{1,0:T(8,128)(2,1)S(1)} %collective-permute-done.2), channel_id=1, source_target_pairs={{0,1},{1,2},{2,3},{3,4},{4,5},{5,6},{6,7},{7,8},{8,9},{9,10},{10,1... | collective-permute-start | bytes 786440 | tf_op jit(solution)/shard_map/ppermute | solution.py:18
  38.3 10.0 %collective-permute-start.5 = (bf16[64,2048]{1,0:T(8,128)(2,1)S(1)}, bf16[64,2048]{1,0:T(8,128)(2,1)S(1)}, u32[]{:S(2)}, u32[]{:S(2)}) collective-permute-start(bf16[64,2048]{1,0:T(8,128)(2,1)S(1)} %collective-permute-done.3), channel_id=1, source_target_pairs={{0,15},{1,0},{2,1},{3,2},{4,3},{5,4},{6,5},{7,6},{8,7},{9,8},{10,9... | collective-permute-start | bytes 786440 | tf_op jit(solution)/shard_map/ppermute | solution.py:23
  48.3 11.2 %collective-permute-start.6 = (bf16[64,2048]{1,0:T(8,128)(2,1)S(1)}, bf16[64,2048]{1,0:T(8,128)(2,1)S(1)}, u32[]{:S(2)}, u32[]{:S(2)}) collective-permute-start(bf16[64,2048]{1,0:T(8,128)(2,1)S(1)} %collective-permute-done.4), channel_id=1, source_target_pairs={{0,1},{1,2},{2,3},{3,4},{4,5},{5,6},{6,7},{7,8},{8,9},{9,10},{10,1... | collective-permute-start | bytes 786440 | tf_op jit(solution)/shard_map/ppermute | solution.py:18
  48.3 11.3 %collective-permute-start.7 = (bf16[64,2048]{1,0:T(8,128)(2,1)S(1)}, bf16[64,2048]{1,0:T(8,128)(2,1)S(1)}, u32[]{:S(2)}, u32[]{:S(2)}) collective-permute-start(bf16[64,2048]{1,0:T(8,128)(2,1)S(1)} %collective-permute-done.5), channel_id=1, source_target_pairs={{0,15},{1,0},{2,1},{3,2},{4,3},{5,4},{6,5},{7,6},{8,7},{9,8},{10,9... | collective-permute-start | bytes 786440 | tf_op jit(solution)/shard_map/ppermute | solution.py:23
  59.5 12.3 %collective-permute-start.8 = (bf16[64,2048]{1,0:T(8,128)(2,1)S(1)}, bf16[64,2048]{1,0:T(8,128)(2,1)S(1)}, u32[]{:S(2)}, u32[]{:S(2)}) collective-permute-start(bf16[64,2048]{1,0:T(8,128)(2,1)S(1)} %collective-permute-done.6), channel_id=1, source_target_pairs={{0,1},{1,2},{2,3},{3,4},{4,5},{5,6},{6,7},{7,8},{8,9},{9,10},{10,1... | collective-permute-start | bytes 786440 | tf_op jit(solution)/shard_map/ppermute | solution.py:18
  59.6 12.4 %collective-permute-start.9 = (bf16[64,2048]{1,0:T(8,128)(2,1)S(1)}, bf16[64,2048]{1,0:T(8,128)(2,1)S(1)}, u32[]{:S(2)}, u32[]{:S(2)}) collective-permute-start(bf16[64,2048]{1,0:T(8,128)(2,1)S(1)} %collective-permute-done.7), channel_id=1, source_target_pairs={{0,15},{1,0},{2,1},{3,2},{4,3},{5,4},{6,5},{7,6},{8,7},{9,8},{10,9... | collective-permute-start | bytes 786440 | tf_op jit(solution)/shard_map/ppermute | solution.py:23
  71.8 11.6 %collective-permute-start.10 = (bf16[64,2048]{1,0:T(8,128)(2,1)S(1)}, bf16[64,2048]{1,0:T(8,128)(2,1)S(1)}, u32[]{:S(2)}, u32[]{:S(2)}) collective-permute-start(bf16[64,2048]{1,0:T(8,128)(2,1)S(1)} %collective-permute-done.8), channel_id=1, source_target_pairs={{0,1},{1,2},{2,3},{3,4},{4,5},{5,6},{6,7},{7,8},{8,9},{9,10},{10,1... | collective-permute-start | bytes 786440 | tf_op jit(solution)/shard_map/ppermute | solution.py:18
  72.0 11.5 %collective-permute-start.11 = (bf16[64,2048]{1,0:T(8,128)(2,1)S(1)}, bf16[64,2048]{1,0:T(8,128)(2,1)S(1)}, u32[]{:S(2)}, u32[]{:S(2)}) collective-permute-start(bf16[64,2048]{1,0:T(8,128)(2,1)S(1)} %collective-permute-done.9), channel_id=1, source_target_pairs={{0,15},{1,0},{2,1},{3,2},{4,3},{5,4},{6,5},{7,6},{8,7},{9,8},{10,9... | collective-permute-start | bytes 786440 | tf_op jit(solution)/shard_map/ppermute | solution.py:23
  83.5 10.8 %collective-permute-start.12 = (bf16[64,2048]{1,0:T(8,128)(2,1)S(1)}, bf16[64,2048]{1,0:T(8,128)(2,1)S(1)}, u32[]{:S(2)}, u32[]{:S(2)}) collective-permute-start(bf16[64,2048]{1,0:T(8,128)(2,1)S(1)} %collective-permute-done.10), channel_id=1, source_target_pairs={{0,1},{1,2},{2,3},{3,4},{4,5},{5,6},{6,7},{7,8},{8,9},{9,10},{10,1... | collective-permute-start | bytes 786440 | tf_op jit(solution)/shard_map/ppermute | solution.py:18
  83.5 10.8 %collective-permute-start.13 = (bf16[64,2048]{1,0:T(8,128)(2,1)S(1)}, bf16[64,2048]{1,0:T(8,128)(2,1)S(1)}, u32[]{:S(2)}, u32[]{:S(2)}) collective-permute-start(bf16[64,2048]{1,0:T(8,128)(2,1)S(1)} %collective-permute-done.11), channel_id=1, source_target_pairs={{0,15},{1,0},{2,1},{3,2},{4,3},{5,4},{6,5},{7,6},{8,7},{9,8},{10,9... | collective-permute-start | bytes 786440 | tf_op jit(solution)/shard_map/ppermute | solution.py:23
  94.2 9.7 %collective-permute-start.14 = (bf16[64,2048]{1,0:T(8,128)(2,1)S(1)}, bf16[64,2048]{1,0:T(8,128)(2,1)S(1)}, u32[]{:S(2)}, u32[]{:S(2)}) collective-permute-start(bf16[64,2048]{1,0:T(8,128)(2,1)S(1)} %collective-permute-done.12), channel_id=1, source_target_pairs={{0,1},{1,2},{2,3},{3,4},{4,5},{5,6},{6,7},{7,8},{8,9},{9,10},{10,1... | collective-permute-start | bytes 786440 | tf_op jit(solution)/shard_map/ppermute | solution.py:18
